TPU v7x, 256 devices: a whole 4x4x8 slice. The times are simulated.
256 devices in a mesh: wide: 32 (over y, x, core), narrow: 8 (over z).
Axes of the slice: x: 4, y: 4, z: 8, core: 2. Of those that a mesh axis runs over, the one named last changes fastest.
Arguments:
- constraint_rows: bfloat16 [512, 256, 1024], P(None, ('wide', 'narrow')), may hold values from -1 to 1
- metric: bfloat16 [1024, 1024], replicated, may hold values from -8 to 8, as said below
Outputs:
- factored: float32 [512, 256, 8, 128], P(None, 'wide', 'narrow')
Inputs may be any that keep to these rules, and one draw needn't show every extreme that they name: `metric`: symmetric and positive definite.
All inputs are finite; a program needn't handle non-finite values.
Results may differ from a plain program's by a relative error of at most 0.0052.
Values may be sent and summed in bfloat16 or wider, within the bound.
No kernel may reach another device: no remote copies, remote signals or barrier semaphores. Data moves between devices by JAX's collectives and lax.ppermute only.
A program may use at most 64 MiB of HBM per device.

v0:
```python
import jax
import jax.numpy as jnp
from jax import lax
from jax.sharding import PartitionSpec as P

P_SIZE = 1024
PB = 256
NPANEL = 2


def left_solve(factor_low, right_side):
    return jax.scipy.linalg.solve_triangular(factor_low, right_side, lower=True)


def strip_major(schur_slab, strips):
    row_count = schur_slab.shape[0]
    strip_len = schur_slab.shape[1] // strips
    reordered = schur_slab.reshape(row_count, strip_len, strips).transpose(0, 2, 1)
    return reordered.reshape(row_count, 1, strips, strip_len)


def local(constraint_rows, metric):
    groups = lax.axis_size(("wide", "narrow"))
    strips = lax.axis_size("narrow")
    row_count = constraint_rows.shape[0]
    panel_depth = P_SIZE // groups
    block_rows = PB // groups
    flat_rows = constraint_rows[:, 0, :]
    projected = jnp.dot(flat_rows, metric, preferred_element_type=jnp.float32).astype(jnp.bfloat16)
    gram_cols = jnp.einsum(
        "rn,kmn->rkm",
        projected,
        lax.all_gather(constraint_rows[:panel_depth], ("wide", "narrow"), axis=1, tiled=True),
        preferred_element_type=jnp.float32,
    )
    schur_slab = (gram_cols * gram_cols).reshape(row_count, P_SIZE)
    grid_block = lax.all_to_all(
        strip_major(schur_slab, strips), "narrow", split_axis=2, concat_axis=1, tiled=True
    )
    strip_len = P_SIZE // strips
    grid_rows = row_count * strips
    narrow_panel = PB // strips
    own_strip = lax.axis_index("narrow")
    flat_block = grid_block.reshape(grid_rows, strip_len)
    for panel_number in range(NPANEL):
        col_begin = panel_number * PB
        row_begin = col_begin // groups
        strip_begin = col_begin // strips
        strip_end = strip_begin + narrow_panel
        own_rows = flat_block.reshape(row_count, strips, strip_len)[
            row_begin : row_begin + block_rows, :, strip_begin:
        ]
        shared = lax.all_gather(own_rows, "wide", axis=1, tiled=True)
        shared = shared.reshape(PB, strip_len - strip_begin)
        diag_strip, row_strip = (
            lax.all_gather(shared[:, :narrow_panel], "narrow", axis=1, tiled=True),
            lax.all_gather(flat_block[:, strip_begin:strip_end], "narrow", axis=1, tiled=True),
        )
        diag_block = diag_strip.reshape(PB, strips, narrow_panel).transpose(0, 2, 1).reshape(PB, PB)
        panel_cols = (
            row_strip.reshape(grid_rows, strips, narrow_panel)
            .transpose(0, 2, 1)
            .reshape(grid_rows, PB)
        )
        factor_low = jnp.linalg.cholesky(diag_block)
        upper_part = left_solve(factor_low, shared[:, narrow_panel:])
        column = left_solve(factor_low, panel_cols.T).T
        trailing = flat_block[:, strip_end:] - jnp.dot(
            column, upper_part, precision=lax.Precision.HIGHEST
        )
        own_cols = lax.dynamic_index_in_dim(
            column.reshape(grid_rows, narrow_panel, strips), own_strip, 2, keepdims=False
        )
        flat_block = jnp.concatenate([flat_block[:, :strip_begin], own_cols, trailing], axis=1)
    return flat_block.reshape(row_count, strips, 1, strip_len)


def solution(mesh):
    placed = (P(None, ("wide", "narrow"), None), P())
    return jax.shard_map(
        local,
        mesh=mesh,
        in_specs=placed,
        out_specs=P(None, "wide", "narrow", None),
        check_vma=False,
    )
```

profile of v0, /device:TPU:4, one launch (start us, length us, event | category | flops | bytes accessed | tf_op | source)
XLA Modules:
  0.0 463.7 jit_solution(18273028846116087548)
XLA Ops:
  6.5 1.5 slice.104
  8.1 110.0 %all-gather.6.cloned.1.call-done = bf16[4,256,1024]{2,0,1:T(4,128)(2,1)} async-done(((bf16[4,1,1024]{2,0,1:T(4,128)(2,1)}), bf16[4,256,1024]{2,0,1:T(4,128)(2,1)}) %all-gather.6.cloned.1.call-update) | async-done | bytes 2097168 | tf_op jit(solution)/shard_map/all_gather | solution.py:33
  118.1 5.7 %fusion.8 = f32[512,4,256]{0,2,1:T(8,128)} fusion(bf16[4,256,1024]{2,0,1:T(4,128)(2,1)} %all-gather.6.cloned.1.call-done, bf16[1024,1024]{1,0:T(8,128)(2,1)S(1)} %copy-done, bf16[512,1,1024]{2,0,1:T(8,128)(2,1)} %param.5), kind=kOutput, calls=%fused_computation.22 | convolution fusion | flops 2148532224 | bytes 7340032 | tf_op jit(solution)/shard_map/rn,kmn->rkm/dot_general | solution.py:30
  123.8 2.0 copy.62
  125.8 56.3 %all_to_all.4 = f32[512,1,8,128]{3,1,0,2:T(1,128)S(1)} all-to-all(f32[512,1,8,128]{3,1,0,2:T(1,128)S(1)} %bitcast.153), channel_id=1, replica_groups=mesh['wide'=32,'narrow'=8] {'narrow'}, dimensions={2} | all-to-all | bytes 4194304 | tf_op jit(solution)/shard_map/all_to_all | solution.py:37
  182.1 1.2 copy.100
  183.4 1.4 copy.68
  184.9 1.9 slice.153
  186.8 23.0 %all-gather = f32[1,1,256,128]{3,2,1,0:T(8,128)S(1)} all-gather(f32[1,1,8,128]{3,2,1,0:T(8,128)S(1)} %bitcast.150), channel_id=2, replica_groups=mesh['wide'=32,'narrow'=8] {'wide'}, dimensions={2}, use_global_device_ids=true | all-gather | bytes 135168 | tf_op jit(solution)/shard_map/all_gather | solution.py:53
  210.1 26.7 %all_gather.23 = f32[256,256]{0,1:T(8,128)S(1)} all-gather(f32[256,32]{0,1:T(8,128)S(1)} %copy.64), channel_id=1, replica_groups=mesh['wide'=32,'narrow'=8] {'narrow'}, dimensions={1}, use_global_device_ids=true | all-gather | bytes 294912 | tf_op jit(solution)/shard_map/all_gather | solution.py:56
  237.3 11.7 %cholesky.130 = f32[128,128]{1,0:T(8,128)S(1)} custom-call(f32[128,128]{1,0:T(8,128)S(1)} %cholesky.194), custom_call_target="Cholesky" | custom-call | tf_op jit(solution)/shard_map/jit(cholesky)/cholesky | solution.py:65
  249.1 9.8 %custom-call.23 = f32[1,128,128]{1,2,0:T(8,128)S(1)} custom-call(f32[1,128,128]{2,1,0:T(8,128)S(1)} %get-tuple-element.66), custom_call_target="InvertDiagBlocksLowerTriangular" | custom-call | tf_op jit(solution)/shard_map/jit(cholesky)/cholesky | solution.py:65
  258.9 0.2 constant_dynamic-update-slice_fusion.2
  259.1 0.3 convolution_subtract_fusion.5
  259.4 11.7 %cholesky.147 = f32[128,128]{1,0:T(8,128)S(1)} custom-call(f32[128,128]{1,0:T(8,128)S(1)} %convolution_subtract_fusion.5), custom_call_target="Cholesky" | custom-call | tf_op jit(solution)/shard_map/jit(cholesky)/cholesky | solution.py:65
  271.2 0.7 compare_reduce_fusion.2
  273.2 3.9 while.6
  273.2 0.6 fusion.60
  273.8 1.3 bitcast_dynamic-update-slice_fusion.4
  275.2 0.6 fusion.60
  275.8 1.3 bitcast_dynamic-update-slice_fusion.4
  277.1 19.7 %custom-call.24 = f32[2,128,128]{1,2,0:T(8,128)S(1)} custom-call(f32[2,128,128]{2,1,0:T(8,128)S(1)} %get-tuple-element.37), custom_call_target="InvertDiagBlocksLowerTriangular" | custom-call | tf_op jit(solution)/shard_map/jit(_solve_triangular)/triangular_solve | solution.py:12
  296.8 2.1 copy.83
  298.9 0.3 fusion.24
  299.3 0.3 convolution_subtract_fusion.6
  299.8 4.6 copy.99
  304.4 1.9 fusion.4
  306.3 2.0 convolution_subtract_fusion.1
  308.3 1.9 fusion.34
  310.3 2.7 convolution_subtract_fusion.2
  313.0 1.1 copy-done.5
  314.2 0.9 slice.156
  315.1 0.9 slice.154
  316.0 24.0 %all-gather.1 = f32[256,96]{1,0:T(8,128)S(1)} all-gather(f32[8,96]{1,0:T(8,128)S(1)} %copy.73), channel_id=3, replica_groups=mesh['wide'=32,'narrow'=8] {'wide'}, dimensions={0}, use_global_device_ids=true | all-gather | bytes 101376 | tf_op jit(solution)/shard_map/all_gather | solution.py:53
  340.2 26.5 %all_gather.26 = f32[256,256]{0,1:T(8,128)S(1)} all-gather(f32[256,32]{0,1:T(8,128)S(1)} %copy.85), channel_id=1, replica_groups=mesh['wide'=32,'narrow'=8] {'narrow'}, dimensions={1}, use_global_device_ids=true | all-gather | bytes 294912 | tf_op jit(solution)/shard_map/all_gather | solution.py:56
  367.2 11.7 %cholesky.164 = f32[128,128]{1,0:T(8,128)S(1)} custom-call(f32[128,128]{1,0:T(8,128)S(1)} %cholesky.197), custom_call_target="Cholesky" | custom-call | tf_op jit(solution)/shard_map/jit(cholesky)/cholesky | solution.py:65
  378.9 9.8 %custom-call.25 = f32[1,128,128]{1,2,0:T(8,128)S(1)} custom-call(f32[1,128,128]{2,1,0:T(8,128)S(1)} %get-tuple-element.62), custom_call_target="InvertDiagBlocksLowerTriangular" | custom-call | tf_op jit(solution)/shard_map/jit(cholesky)/cholesky | solution.py:65
  388.8 0.2 constant_dynamic-update-slice_fusion
  389.0 0.3 convolution_subtract_fusion.4
  389.3 11.7 %cholesky.181 = f32[128,128]{1,0:T(8,128)S(1)} custom-call(f32[128,128]{1,0:T(8,128)S(1)} %convolution_subtract_fusion.4), custom_call_target="Cholesky" | custom-call | tf_op jit(solution)/shard_map/jit(cholesky)/cholesky | solution.py:65
  401.0 0.6 compare_reduce_fusion.1
  401.7 0.7 compare_reduce_fusion
  403.6 3.9 while.7
  403.6 0.6 fusion.61
  404.2 1.3 bitcast_dynamic-update-slice_fusion.5
  405.6 0.6 fusion.61
  406.2 1.3 bitcast_dynamic-update-slice_fusion.5
  407.5 19.7 %custom-call.26 = f32[2,128,128]{1,2,0:T(8,128)S(1)} custom-call(f32[2,128,128]{2,1,0:T(8,128)S(1)} %get-tuple-element.38), custom_call_target="InvertDiagBlocksLowerTriangular" | custom-call | tf_op jit(solution)/shard_map/jit(_solve_triangular)/triangular_solve | solution.py:12
  427.2 2.0 fusion.1
  429.2 0.5 constant_dynamic-slice_fusion.3
  429.7 1.9 copy.70
  431.7 0.3 fusion.20
  432.0 0.2 convolution_subtract_fusion.7
  432.5 4.6 copy.98
  437.1 1.9 fusion.2
  439.0 2.0 convolution_subtract_fusion
  441.0 1.9 fusion.36
  443.0 0.4 fusion
  443.4 1.0 copy-done.6
  444.4 2.9 convolution_subtract_fusion.3
  447.2 0.5 constant_dynamic-slice_fusion.2
  447.7 2.0 copy.80
  449.7 1.7 copy.78
  451.5 5.5 %pad_maximum_fusion.4 = f32[512,8,1,128]{3,1,0,2:T(8,128)} fusion(f32[512,8,1,64]{3,1,0,2:T(8,128)} %bitcast.154, f32[512,8,1,32]{3,1,0,2:T(8,128)} %bitcast.152, f32[512,8,1,32]{3,1,0,2:T(8,128)} %bitcast.151), kind=kLoop, calls=%fused_computation.18 | loop fusion | flops 1048576 | bytes 4194304 | tf_op jit(solution)/shard_map/concatenate | solution.py:74
  (57 shorter events, 2.5 us)
Async XLA Ops:
  6.5 111.6 %copy-start = (bf16[1024,1024]{1,0:T(8,128)(2,1)S(1)}, bf16[1024,1024]{1,0:T(8,128)(2,1)}, u32[]{:S(2)}) copy-start(bf16[1024,1024]{1,0:T(8,128)(2,1)} %param.6) | copy-start | bytes 6291460
  6.5 111.6 %all-gather.6.cloned.1.call-start = ((), (), s32[]{:S(2)}) async-start(), calls=%async_computation.1 | async-start | bytes 2105344 | tf_op jit(solution)/shard_map/all_gather | solution.py:33
  8.0 291.7 %all-gather.8.cloned.1.call-start = ((), (), s32[]{:S(2)}) async-start(), calls=%async_computation.2 | async-start | bytes 4718592 | tf_op jit(solution)/shard_map/all_gather | solution.py:57
  182.1 1.3 copy-start.3
  184.8 247.6 %all-gather.10.cloned.1.call-start = ((), (), s32[]{:S(2)}) async-start(), calls=%async_computation.3 | async-start | bytes 4718592 | tf_op jit(solution)/shard_map/all_gather | solution.py:57
  184.9 1.9 slice-start
  237.0 59.8 %copy-start.4 = (f32[4096,96]{1,0:T(8,128)S(1)}, f32[4096,96]{1,0:T(8,128)}, u32[]{:S(2)}) copy-start(f32[4096,96]{1,0:T(8,128)} %slice.153) | copy-start | bytes 4718596
  308.3 2.0 copy-start.7
  310.3 2.8 copy-start.2
  313.0 1.1 copy-start.5
  442.9 1.4 copy-start.6
  451.5 5.5 %copy-start.1 = (bf16[1024,1024]{1,0:T(8,128)(2,1)S(1)}, bf16[1024,1024]{1,0:T(8,128)(2,1)}, u32[]{:S(2)}) copy-start(bf16[1024,1024]{1,0:T(8,128)(2,1)} %param.6) | copy-start | bytes 6291460
Sparse Core Ops, SparseCore 0:
  11.1 107.0 all-gather.5
  184.9 53.2 all-gather.7
  315.2 53.6 all-gather.9
where the time goes:
time: 469 us; the launch traced here: 464 us
  blocking collectives  157 us (33%)
  other arithmetic  116 us (25%)
  waiting for transfers between devices  110 us (23%)
  local copies, waits for them, and re-layouts  38.8 us (8%)
  matrix products  25.5 us (5%)
  between operations  16.2 us (3%)
    all_gather x1, waiting for transfers between devices, local(): lax.all_gather(constraint_rows[:panel_depth], ('wide', 'narrow'), axis=1,...  110 us
    another operation x13, other arithmetic, local(): factor_low = jnp.linalg.cholesky(diag_block)  68.6 us
    all_to_all x1, blocking collectives, local(): lax.all_to_all(strip_major(schur_slab, strips), 'narrow', split_axis=2, c...  56.3 us
    all_gather x2, blocking collectives, local(): lax.all_gather(shared[:, :narrow_panel], 'narrow', axis=1, tiled=True)  53.2 us
    all_gather x2, blocking collectives, local(): shared = lax.all_gather(own_rows, 'wide', axis=1, tiled=True)  47 us
    another operation x5, other arithmetic, left_solve(): return jax.scipy.linalg.solve_triangular(factor_low, right_side, lower=True)  39.4 us
    another operation x12, matrix products, left_solve(): return jax.scipy.linalg.solve_triangular(factor_low, right_side, lower=True)  13.2 us
  transfers between devices with their start and end apart: 3, of which 1 were waited for; matrix products, arithmetic and copies ran while one was open for 28% of the time, Pallas kernels for 0%

commit v1 on v0

--- a/solution.py
+++ b/solution.py
@@ -6,6 +6,9 @@
 P_SIZE = 1024
 PB = 256
 NPANEL = 2
+flows_note = lambda frame: jnp.concatenate(
+    lax.all_to_all(jnp.stack(lax.psum(1, "wide") * [frame]), "wide", 0, 0), axis=1
+)
 
 
 def left_solve(factor_low, right_side):
@@ -50,7 +53,7 @@
         own_rows = flat_block.reshape(row_count, strips, strip_len)[
             row_begin : row_begin + block_rows, :, strip_begin:
         ]
-        shared = lax.all_gather(own_rows, "wide", axis=1, tiled=True)
+        shared = flows_note(own_rows)
         shared = shared.reshape(PB, strip_len - strip_begin)
         diag_strip, row_strip = (
             lax.all_gather(shared[:, :narrow_panel], "narrow", axis=1, tiled=True),

time: 469 us -> 442 us (0.942)
  blocking collectives: 157 us -> 110 us
  starting transfers between devices: 0.09 us -> 14.2 us
    all_gather x2 -> x0, blocking collectives: 47 us -> none  [local(): shared = lax.all_gather(own_rows, 'wide', axis=1, tiled=True)]
    all_to_all x0 -> x2, starting transfers between devices: none -> 14.1 us  [lax.all_to_all(jnp.stack(lax.psum(1, 'wide') * [frame]), 'wide', 0, 0)]
  transfers between devices with their start and end apart: 3 -> 5, of which waited for: 1 -> 3; matrix products, arithmetic and copies ran while one was open for 28% -> 30% of each run, Pallas kernels for 0% -> 0%
where the time goes in v1:
time: 442 us; the launch traced here: 436 us
  other arithmetic  117 us (26%)
  waiting for transfers between devices  112 us (25%)
  blocking collectives  110 us (25%)
  local copies, waits for them, and re-layouts  40.9 us (9%)
  matrix products  25.5 us (6%)
  between operations  16.4 us (4%)
  starting transfers between devices  14.2 us (3%)
    all_gather x1, waiting for transfers between devices, local(): lax.all_gather(constraint_rows[:panel_depth], ('wide', 'narrow'), axis=1,...  110 us
    another operation x13, other arithmetic, local(): factor_low = jnp.linalg.cholesky(diag_block)  68.6 us
    all_to_all x1, blocking collectives, local(): lax.all_to_all(strip_major(schur_slab, strips), 'narrow', split_axis=2, c...  56.3 us
    all_gather x2, blocking collectives, local(): lax.all_gather(shared[:, :narrow_panel], 'narrow', axis=1, tiled=True)  53.3 us
    another operation x5, other arithmetic, left_solve(): return jax.scipy.linalg.solve_triangular(factor_low, right_side, lower=True)  40 us
    all_to_all x2, starting transfers between devices, lax.all_to_all(jnp.stack(lax.psum(1, 'wide') * [frame]), 'wide', 0, 0)  14.1 us
    another operation x12, matrix products, left_solve(): return jax.scipy.linalg.solve_triangular(factor_low, right_side, lower=True)  13.2 us
  transfers between devices with their start and end apart: 5, of which 3 were waited for; matrix products, arithmetic and copies ran while one was open for 30% of the time, Pallas kernels for 0%

profile of v1, /device:TPU:4, one launch (start us, length us, event | category | flops | bytes accessed | tf_op | source)
XLA Modules:
  0.0 435.6 jit_solution(18240408538784316189)
XLA Ops:
  6.5 1.5 slice.100
  8.1 110.0 %all-gather.4.cloned.1.call-done = bf16[4,256,1024]{2,0,1:T(4,128)(2,1)} async-done(((bf16[4,1,1024]{2,0,1:T(4,128)(2,1)}), bf16[4,256,1024]{2,0,1:T(4,128)(2,1)}) %all-gather.4.cloned.1.call-update) | async-done | bytes 2097168 | tf_op jit(solution)/shard_map/all_gather | solution.py:36
  118.1 5.7 %fusion.8 = f32[512,4,256]{0,2,1:T(8,128)} fusion(bf16[4,256,1024]{2,0,1:T(4,128)(2,1)} %all-gather.4.cloned.1.call-done, bf16[1024,1024]{1,0:T(8,128)(2,1)S(1)} %copy-done, bf16[512,1,1024]{2,0,1:T(8,128)(2,1)} %param.5), kind=kOutput, calls=%fused_computation.22 | convolution fusion | flops 2148532224 | bytes 7340032 | tf_op jit(solution)/shard_map/rn,kmn->rkm/dot_general | solution.py:33
  123.8 2.0 copy.46
  125.8 56.3 %all_to_all.19 = f32[512,1,8,128]{3,1,0,2:T(1,128)S(1)} all-to-all(f32[512,1,8,128]{3,1,0,2:T(1,128)S(1)} %bitcast.156), channel_id=1, replica_groups=mesh['wide'=32,'narrow'=8] {'narrow'}, dimensions={2} | all-to-all | bytes 4194304 | tf_op jit(solution)/shard_map/all_to_all | solution.py:40
  182.1 1.2 copy.83
  183.4 1.4 copy.52
  184.8 0.7 stack.7
  185.5 7.3 %all-to-all-start.1 = ((f32[32,1,8,128]{3,2,1,0:T(8,128)}), f32[32,1,8,128]{3,2,1,0:T(8,128)S(1)}, u32[]{:S(2)}, u32[]{:S(2)}) async-start(f32[32,1,8,128]{3,2,1,0:T(8,128)} %stack.7), calls=%async_computation.1 | async-start | bytes 262144 | tf_op jit(solution)/shard_map/all_to_all | solution.py:10
  192.9 1.9 slice.147
  194.8 2.8 copy.67
  197.5 0.8 all-to-all-done.1
  198.6 26.7 %all_gather.16 = f32[256,256]{0,1:T(8,128)S(1)} all-gather(f32[256,32]{0,1:T(8,128)S(1)} %copy.48), channel_id=1, replica_groups=mesh['wide'=32,'narrow'=8] {'narrow'}, dimensions={1}, use_global_device_ids=true | all-gather | bytes 294912 | tf_op jit(solution)/shard_map/all_gather | solution.py:59
  225.8 11.7 %cholesky.130 = f32[128,128]{1,0:T(8,128)S(1)} custom-call(f32[128,128]{1,0:T(8,128)S(1)} %cholesky.194), custom_call_target="Cholesky" | custom-call | tf_op jit(solution)/shard_map/jit(cholesky)/cholesky | solution.py:68
  237.5 9.8 %custom-call.23 = f32[1,128,128]{1,2,0:T(8,128)S(1)} custom-call(f32[1,128,128]{2,1,0:T(8,128)S(1)} %get-tuple-element.66), custom_call_target="InvertDiagBlocksLowerTriangular" | custom-call | tf_op jit(solution)/shard_map/jit(cholesky)/cholesky | solution.py:68
  247.6 0.3 convolution_subtract_fusion.5
  247.9 11.7 %cholesky.147 = f32[128,128]{1,0:T(8,128)S(1)} custom-call(f32[128,128]{1,0:T(8,128)S(1)} %convolution_subtract_fusion.5), custom_call_target="Cholesky" | custom-call | tf_op jit(solution)/shard_map/jit(cholesky)/cholesky | solution.py:68
  259.6 0.7 compare_reduce_fusion.2
  261.7 4.0 while.6
  261.7 0.6 fusion.60
  262.3 1.4 bitcast_dynamic-update-slice_fusion.4
  263.7 0.6 fusion.60
  264.3 1.4 bitcast_dynamic-update-slice_fusion.4
  265.7 20.1 %custom-call.24 = f32[2,128,128]{1,2,0:T(8,128)S(1)} custom-call(f32[2,128,128]{2,1,0:T(8,128)S(1)} %get-tuple-element.37), custom_call_target="InvertDiagBlocksLowerTriangular" | custom-call | tf_op jit(solution)/shard_map/jit(_solve_triangular)/triangular_solve | solution.py:15
  285.8 0.3 fusion.24
  286.6 4.6 %copy.82 = f32[4096,32,8]{0,2,1:T(8,128)S(1)} copy(f32[4096,32,8]{0,1,2:T(8,128)} %bitcast.159) | data formatting | bytes 8388608 | tf_op jit(solution)/shard_map/transpose | solution.py:65
  291.2 1.9 fusion.4
  293.2 2.0 convolution_subtract_fusion.1
  295.2 1.9 fusion.34
  297.1 2.7 convolution_subtract_fusion.2
  299.9 1.1 copy-done.4
  301.0 0.9 slice.150
  301.9 0.9 slice.148
  302.9 0.7 stack.8
  303.6 6.8 %all-to-all-start.2 = ((f32[32,1,8,96]{3,2,1,0:T(8,128)}), f32[32,1,8,96]{3,2,1,0:T(8,128)S(1)}, u32[]{:S(2)}, u32[]{:S(2)}) async-start(f32[32,1,8,96]{3,2,1,0:T(8,128)} %stack.8), calls=%async_computation.2 | async-start | bytes 262144 | tf_op jit(solution)/shard_map/all_to_all | solution.py:10
  310.4 2.0 fusion.1
  312.4 0.5 constant_dynamic-slice_fusion.3
  312.9 1.8 copy.54
  314.7 1.1 all-to-all-done.2
  316.0 26.6 %all_gather.18 = f32[256,256]{0,1:T(8,128)S(1)} all-gather(f32[256,32]{0,1:T(8,128)S(1)} %copy.58), channel_id=1, replica_groups=mesh['wide'=32,'narrow'=8] {'narrow'}, dimensions={1}, use_global_device_ids=true | all-gather | bytes 294912 | tf_op jit(solution)/shard_map/all_gather | solution.py:59
  343.0 11.7 %cholesky.164 = f32[128,128]{1,0:T(8,128)S(1)} custom-call(f32[128,128]{1,0:T(8,128)S(1)} %cholesky.197), custom_call_target="Cholesky" | custom-call | tf_op jit(solution)/shard_map/jit(cholesky)/cholesky | solution.py:68
  354.8 9.8 %custom-call.25 = f32[1,128,128]{1,2,0:T(8,128)S(1)} custom-call(f32[1,128,128]{2,1,0:T(8,128)S(1)} %get-tuple-element.62), custom_call_target="InvertDiagBlocksLowerTriangular" | custom-call | tf_op jit(solution)/shard_map/jit(cholesky)/cholesky | solution.py:68
  364.9 0.3 convolution_subtract_fusion.4
  365.1 11.7 %cholesky.181 = f32[128,128]{1,0:T(8,128)S(1)} custom-call(f32[128,128]{1,0:T(8,128)S(1)} %convolution_subtract_fusion.4), custom_call_target="Cholesky" | custom-call | tf_op jit(solution)/shard_map/jit(cholesky)/cholesky | solution.py:68
  376.8 0.6 compare_reduce_fusion.1
  377.5 0.7 compare_reduce_fusion
  379.6 4.1 while.7
  379.6 0.6 fusion.61
  380.2 1.4 bitcast_dynamic-update-slice_fusion.5
  381.7 0.6 fusion.61
  382.2 1.4 bitcast_dynamic-update-slice_fusion.5
  383.7 19.9 %custom-call.26 = f32[2,128,128]{1,2,0:T(8,128)S(1)} custom-call(f32[2,128,128]{2,1,0:T(8,128)S(1)} %get-tuple-element.38), custom_call_target="InvertDiagBlocksLowerTriangular" | custom-call | tf_op jit(solution)/shard_map/jit(_solve_triangular)/triangular_solve | solution.py:15
  403.6 0.3 fusion.20
  404.4 4.6 %copy.81 = f32[4096,8,32]{0,1,2:T(8,128)S(1)} copy(f32[4096,8,32]{0,2,1:T(8,128)} %bitcast.158) | data formatting | bytes 8388608 | tf_op jit(solution)/shard_map/reshape | solution.py:64
  409.0 1.9 fusion.2
  410.9 2.0 convolution_subtract_fusion
  412.9 1.9 fusion.36
  414.9 0.4 fusion
  415.3 1.0 copy-done.5
  416.3 2.9 convolution_subtract_fusion.3
  419.2 0.5 constant_dynamic-slice_fusion.2
  419.7 1.9 copy.64
  421.6 1.7 copy.62
  423.4 5.5 %pad_maximum_fusion.4 = f32[512,8,1,128]{3,1,0,2:T(8,128)} fusion(f32[512,8,1,64]{3,1,0,2:T(8,128)} %bitcast.157, f32[512,8,1,32]{3,1,0,2:T(8,128)} %bitcast.155, f32[512,8,1,32]{3,1,0,2:T(8,128)} %bitcast.154), kind=kLoop, calls=%fused_computation.18 | loop fusion | flops 1048576 | bytes 4194304 | tf_op jit(solution)/shard_map/concatenate | solution.py:77
  (59 shorter events, 3.4 us)
Async XLA Ops:
  6.5 111.6 %copy-start = (bf16[1024,1024]{1,0:T(8,128)(2,1)S(1)}, bf16[1024,1024]{1,0:T(8,128)(2,1)}, u32[]{:S(2)}) copy-start(bf16[1024,1024]{1,0:T(8,128)(2,1)} %param.6) | copy-start | bytes 6291460
  6.5 111.6 %all-gather.4.cloned.1.call-start = ((), (), s32[]{:S(2)}) async-start(), calls=%async_computation.3 | async-start | bytes 2105344 | tf_op jit(solution)/shard_map/all_gather | solution.py:36
  8.0 278.6 %all-gather.6.cloned.1.call-start = ((), (), s32[]{:S(2)}) async-start(), calls=%async_computation.4 | async-start | bytes 4718592 | tf_op jit(solution)/shard_map/all_gather | solution.py:60
  182.1 1.3 copy-start.3
  183.4 1.4 slice-start
  185.5 12.9 %all-to-all-start.1 = ((f32[32,1,8,128]{3,2,1,0:T(8,128)}), f32[32,1,8,128]{3,2,1,0:T(8,128)S(1)}, u32[]{:S(2)}, u32[]{:S(2)}) async-start(f32[32,1,8,128]{3,2,1,0:T(8,128)} %stack.7), calls=%async_computation.1 | async-start | bytes 262144 | tf_op jit(solution)/shard_map/all_to_all | solution.py:10
  192.8 211.6 %all-gather.8.cloned.1.call-start = ((), (), s32[]{:S(2)}) async-start(), calls=%async_computation.5 | async-start | bytes 4718592 | tf_op jit(solution)/shard_map/all_gather | solution.py:60
  295.1 2.0 copy-start.6
  297.1 2.8 copy-start.2
  299.9 1.2 copy-start.4
  303.6 12.2 %all-to-all-start.2 = ((f32[32,1,8,96]{3,2,1,0:T(8,128)}), f32[32,1,8,96]{3,2,1,0:T(8,128)S(1)}, u32[]{:S(2)}, u32[]{:S(2)}) async-start(f32[32,1,8,96]{3,2,1,0:T(8,128)} %stack.8), calls=%async_computation.2 | async-start | bytes 262144 | tf_op jit(solution)/shard_map/all_to_all | solution.py:10
  414.9 1.4 copy-start.5
  423.4 5.5 %copy-start.1 = (bf16[1024,1024]{1,0:T(8,128)(2,1)S(1)}, bf16[1024,1024]{1,0:T(8,128)(2,1)}, u32[]{:S(2)}) copy-start(bf16[1024,1024]{1,0:T(8,128)(2,1)} %param.6) | copy-start | bytes 6291460
Sparse Core Ops, SparseCore 0:
  11.1 107.0 all-gather.3
  184.9 53.5 all-gather.5
  302.1 53.6 all-gather.7
